TPU v7x, 32 devices: a whole 2x2x4 slice. The times are simulated.
32 devices in a mesh: fsdp: 8 (over z, y), seq: 4 (over x, core).
Axes of the slice: x: 2, y: 2, z: 4, core: 2. Of those that a mesh axis runs over, the one named last changes fastest.
Arguments:
- activations: bfloat16 [8, 2560, 1024], P('fsdp', 'seq'), may hold values from -6 to 6
- cotangent: bfloat16 [8, 2560, 1024], P('fsdp', 'seq'), may hold values from -6 to 6
- gain_attn: bfloat16 [1024], P('fsdp'), may hold values from 0.25 to 1.75
- w_qkv: bfloat16 [1024, 3072], P('fsdp'), may hold values from -0.25 to 0.25
- w_attn_out: bfloat16 [1024, 1024], P('fsdp'), may hold values from -0.75 to 0.75
- gain_mlp: bfloat16 [1024], P('fsdp'), may hold values from 0.25 to 1.75
- w_in: bfloat16 [1024, 5248], P('fsdp'), may hold values from -0.1875 to 0.1875
- w_mlp_out: bfloat16 [2624, 1024], P('fsdp'), may hold values from -0.125 to 0.125
Outputs:
- output: bfloat16 [8, 2560, 1024], P('fsdp', 'seq')
- d_input: bfloat16 [8, 2560, 1024], P('fsdp', 'seq')
- grad_gain_attn: float32 [1024], P('fsdp')
- grad_gain_mlp: float32 [1024], P('fsdp')
- grad_w_qkv: float32 [1024, 3072], P('fsdp')
- grad_w_attn_out: float32 [1024, 1024], P('fsdp')
- grad_w_in: float32 [1024, 5248], P('fsdp')
- grad_w_mlp_out: float32 [2624, 1024], P('fsdp')
All inputs are finite; a program needn't handle non-finite values.
Results may differ from a plain program's by a relative error of at most 0.023.
Values may be sent and summed in bfloat16 or wider, within the bound.
No kernel may reach another device: no remote copies, remote signals or barrier semaphores. Data moves between devices by JAX's collectives and lax.ppermute only.
A program may use at most 192 MiB of HBM per device.

v0:
```python
import math
import jax
import jax.numpy as jnp
from jax import lax
from jax.sharding import PartitionSpec as P

HEADS = 16
HEAD = 64
FF = 2624
LENGTH = 2560
QB = 512
eps = 1e-05
rope_base = 160000.0


def layer_norm(values, gain_vec):
    average = jnp.mean(values, -1, keepdims=True)
    centred = values - average
    variance = jnp.mean(centred * centred, -1, keepdims=True)
    return centred * lax.rsqrt(variance + eps) * gain_vec


def gelu_exact(values):
    return 0.5 * values * (1.0 + lax.erf(values * 2.0 ** (-0.5)))


def rope_tables(positions):
    half_size = HEAD // 2
    freq_index = jnp.arange(half_size).astype(positions.dtype)
    inverse = jnp.exp(freq_index * (-2.0 * math.log(rope_base) / HEAD))
    angles = positions[:, None] * inverse[None, :]
    angles = jnp.concatenate([angles, angles], 1)
    return (jnp.cos(angles), jnp.sin(angles))


def rotate(tensor, cosine, sine_table):
    half_size = HEAD // 2
    first = tensor[..., :half_size]
    second = tensor[..., half_size:]
    turned = jnp.concatenate([-second, first], -1)
    return tensor * cosine + turned * sine_table


def contract_rows(left, right):
    return lax.dot_general(
        left, right, (((0,), (0,)), ((), ())), preferred_element_type=jnp.float32
    )


def times_transpose(left, right):
    return lax.dot_general(
        left, right, (((1,), (1,)), ((), ())), preferred_element_type=jnp.float32
    )


def split_heads(packed_heads):
    local_heads = packed_heads.shape[2] // HEAD
    queries = packed_heads[:, 0].reshape(LENGTH // QB, QB, local_heads, HEAD)
    key_rows = packed_heads[:, 1].reshape(LENGTH, local_heads, HEAD)
    value_rows = packed_heads[:, 2].reshape(LENGTH, local_heads, HEAD)
    return (local_heads, queries, key_rows, value_rows)


def attend_sequence(packed_heads):
    local_heads, queries, key_rows, value_rows = split_heads(packed_heads)
    factor = float(HEAD) ** (-0.5)

    def one_block(q_block):
        scores = (
            jnp.einsum("qhd,khd->hqk", q_block, key_rows, preferred_element_type=jnp.float32)
            * factor
        )
        row_peak = jnp.max(scores, -1, keepdims=True)
        exponent = jnp.exp(scores - row_peak)
        row_total = jnp.sum(exponent, -1, keepdims=True)
        probs = (exponent / row_total).astype(jnp.bfloat16)
        attended = jnp.einsum("hqk,khd->qhd", probs, value_rows, preferred_element_type=jnp.float32)
        attended = attended.astype(jnp.bfloat16).reshape(QB, local_heads * HEAD)
        return (attended, (row_peak + jnp.log(row_total))[..., 0])

    attended, log_sums = lax.map(one_block, queries)
    return (attended.reshape(LENGTH, local_heads * HEAD), log_sums)


def attend_backward(pieces):
    packed_heads, log_sums, grad_heads = pieces
    local_heads, queries, key_rows, value_rows = split_heads(packed_heads)
    factor = float(HEAD) ** (-0.5)
    grad_blocks = grad_heads.reshape(LENGTH // QB, QB, local_heads, HEAD)

    def one_block(carry, block_pieces):
        key_grad, value_grad = carry
        q_block, lse_block, g_block = block_pieces
        scores = (
            jnp.einsum("qhd,khd->hqk", q_block, key_rows, preferred_element_type=jnp.float32)
            * factor
        )
        probs = jnp.exp(scores - lse_block[..., None])
        value_grad = value_grad + jnp.einsum(
            "hqk,qhd->khd", probs.astype(jnp.bfloat16), g_block, preferred_element_type=jnp.float32
        )
        prob_grad = jnp.einsum(
            "qhd,khd->hqk", g_block, value_rows, preferred_element_type=jnp.float32
        )
        inner = jnp.sum(probs * prob_grad, -1, keepdims=True)
        score_grad = (probs * (prob_grad - inner)).astype(jnp.bfloat16)
        query_grad = (
            jnp.einsum("hqk,khd->qhd", score_grad, key_rows, preferred_element_type=jnp.float32)
            * factor
        )
        key_grad = (
            key_grad
            + jnp.einsum("hqk,qhd->khd", score_grad, q_block, preferred_element_type=jnp.float32)
            * factor
        )
        return ((key_grad, value_grad), query_grad)

    zeros_state = jnp.zeros((LENGTH, local_heads, HEAD), jnp.float32)
    (key_grad, value_grad), query_grad = lax.scan(
        one_block, (zeros_state, zeros_state), (queries, log_sums, grad_blocks)
    )
    width_local = local_heads * HEAD
    stacked = jnp.stack(
        [
            query_grad.reshape(LENGTH, width_local),
            key_grad.reshape(LENGTH, width_local),
            value_grad.reshape(LENGTH, width_local),
        ],
        1,
    )
    return stacked.astype(jnp.bfloat16)


def local(activations, cotangent, gain_attn, w_qkv, w_attn_out, gain_mlp, w_in, w_mlp_out):
    local_seqs, positions, width = activations.shape
    row_count = local_seqs * positions
    gathered = (
        lax.all_gather(gain_attn, "fsdp", axis=0, tiled=True),
        lax.all_gather(w_qkv, "fsdp", axis=0, tiled=True),
        lax.all_gather(w_attn_out, "fsdp", axis=0, tiled=True),
        lax.all_gather(gain_mlp, "fsdp", axis=0, tiled=True),
        lax.all_gather(w_in, "fsdp", axis=0, tiled=True),
        lax.all_gather(w_mlp_out, "fsdp", axis=0, tiled=True),
    )
    full_gain_attn, full_qkv, full_attn_out, full_gain_mlp, full_in, full_mlp_out = gathered
    tokens = activations.astype(jnp.float32).reshape(row_count, width)
    normed, first_back = jax.vjp(layer_norm, tokens, full_gain_attn.astype(jnp.float32))
    normed_low = normed.astype(jnp.bfloat16)
    packed = jnp.dot(normed_low, full_qkv, preferred_element_type=jnp.float32)
    packed = packed.reshape(local_seqs, positions, 3, HEADS, HEAD)
    starting = (lax.axis_index("seq") * positions).astype(jnp.float32)
    places = starting + jnp.arange(positions).astype(jnp.float32)
    cosine, sine_table = rope_tables(places)

    def turn_pair(pair_values):
        return rotate(pair_values, cosine[:, None, None, :], sine_table[:, None, None, :])

    turned, turn_back = jax.vjp(turn_pair, packed[:, :, :2])
    rotated = jnp.concatenate([turned, packed[:, :, 2:]], 2).astype(jnp.bfloat16)
    rotated = rotated.reshape(local_seqs, positions, 3, width)
    heads_layout = lax.all_to_all(rotated, "seq", split_axis=3, concat_axis=1, tiled=True)
    attended_heads, log_sums = lax.map(attend_sequence, heads_layout)
    attended = lax.all_to_all(attended_heads, "seq", split_axis=1, concat_axis=2, tiled=True)
    attended_rows = attended.reshape(row_count, width)
    mixed = tokens + jnp.dot(attended_rows, full_attn_out, preferred_element_type=jnp.float32)
    normed_mlp, norm_back = jax.vjp(layer_norm, mixed, full_gain_mlp.astype(jnp.float32))
    normed_mlp_low = normed_mlp.astype(jnp.bfloat16)
    gate_up = jnp.dot(normed_mlp_low, full_in, preferred_element_type=jnp.float32)

    def gated(gate_part, up_part):
        return gelu_exact(gate_part) * up_part

    hidden, gated_back = jax.vjp(gated, gate_up[:, :FF], gate_up[:, FF:])
    hidden_low = hidden.astype(jnp.bfloat16)
    result = mixed + jnp.dot(hidden_low, full_mlp_out, preferred_element_type=jnp.float32)
    output = result.astype(jnp.bfloat16).reshape(activations.shape)
    again = (
        lax.all_gather(w_qkv, "fsdp", axis=0, tiled=True),
        lax.all_gather(w_attn_out, "fsdp", axis=0, tiled=True),
        lax.all_gather(w_in, "fsdp", axis=0, tiled=True),
        lax.all_gather(w_mlp_out, "fsdp", axis=0, tiled=True),
    )
    again_qkv, again_attn_out, again_in, again_mlp_out = again
    out_grad = cotangent.reshape(row_count, width)
    grad_mlp_out = contract_rows(hidden_low, out_grad)
    hidden_grad = times_transpose(out_grad, again_mlp_out)
    gate_grad, up_grad = gated_back(hidden_grad)
    gate_up_grad = jnp.concatenate([gate_grad, up_grad], 1).astype(jnp.bfloat16)
    grad_in = contract_rows(normed_mlp_low, gate_up_grad)
    normed_mlp_grad = times_transpose(gate_up_grad, again_in)
    mixed_grad_norm, grad_gain_mlp = norm_back(normed_mlp_grad)
    mixed_grad = out_grad.astype(jnp.float32) + mixed_grad_norm
    mixed_low = mixed_grad.astype(jnp.bfloat16)
    grad_attn_out = contract_rows(attended_rows, mixed_low)
    attended_grad = times_transpose(mixed_low, again_attn_out).astype(jnp.bfloat16)
    attended_grad = attended_grad.reshape(local_seqs, positions, width)
    grad_heads = lax.all_to_all(attended_grad, "seq", split_axis=2, concat_axis=1, tiled=True)
    rotated_grad = lax.map(attend_backward, (heads_layout, log_sums, grad_heads))
    position_grad = lax.all_to_all(rotated_grad, "seq", split_axis=1, concat_axis=3, tiled=True)
    position_grad = position_grad.astype(jnp.float32).reshape(local_seqs, positions, 3, HEADS, HEAD)
    (pair_grad,) = turn_back(position_grad[:, :, :2])
    packed_grad = jnp.concatenate([pair_grad, position_grad[:, :, 2:]], 2).astype(jnp.bfloat16)
    packed_grad = packed_grad.reshape(row_count, 3 * width)
    grad_qkv = contract_rows(normed_low, packed_grad)
    normed_grad = times_transpose(packed_grad, again_qkv)
    token_grad_norm, grad_gain_attn = first_back(normed_grad)
    d_input = (mixed_grad + token_grad_norm).astype(jnp.bfloat16).reshape(activations.shape)
    gradients = (grad_gain_attn, grad_gain_mlp, grad_qkv, grad_attn_out, grad_in, grad_mlp_out)
    shards = (
        lax.psum_scatter(
            gradients[0].astype(jnp.bfloat16), "fsdp", scatter_dimension=0, tiled=True
        ).astype(jnp.float32),
        lax.psum_scatter(
            gradients[1].astype(jnp.bfloat16), "fsdp", scatter_dimension=0, tiled=True
        ).astype(jnp.float32),
        lax.psum_scatter(
            gradients[2].astype(jnp.bfloat16), "fsdp", scatter_dimension=0, tiled=True
        ).astype(jnp.float32),
        lax.psum_scatter(
            gradients[3].astype(jnp.bfloat16), "fsdp", scatter_dimension=0, tiled=True
        ).astype(jnp.float32),
        lax.psum_scatter(
            gradients[4].astype(jnp.bfloat16), "fsdp", scatter_dimension=0, tiled=True
        ).astype(jnp.float32),
        lax.psum_scatter(
            gradients[5].astype(jnp.bfloat16), "fsdp", scatter_dimension=0, tiled=True
        ).astype(jnp.float32),
    )
    shards = (
        lax.psum(shards[0].astype(jnp.bfloat16), "seq").astype(jnp.float32),
        lax.psum(shards[1].astype(jnp.bfloat16), "seq").astype(jnp.float32),
        lax.psum(shards[2].astype(jnp.bfloat16), "seq").astype(jnp.float32),
        lax.psum(shards[3].astype(jnp.bfloat16), "seq").astype(jnp.float32),
        lax.psum(shards[4].astype(jnp.bfloat16), "seq").astype(jnp.float32),
        lax.psum(shards[5].astype(jnp.bfloat16), "seq").astype(jnp.float32),
    )
    return (output, d_input, shards[0], shards[1], shards[2], shards[3], shards[4], shards[5])


def solution(mesh):
    in_specs = (
        P("fsdp", "seq", None),
        P("fsdp", "seq", None),
        P("fsdp"),
        P("fsdp", None),
        P("fsdp", None),
        P("fsdp"),
        P("fsdp", None),
        P("fsdp", None),
    )
    out_specs = (
        P("fsdp", "seq", None),
        P("fsdp", "seq", None),
        P("fsdp"),
        P("fsdp"),
        P("fsdp", None),
        P("fsdp", None),
        P("fsdp", None),
        P("fsdp", None),
    )
    return jax.shard_map(local, mesh=mesh, in_specs=in_specs, out_specs=out_specs, check_vma=False)
```

profile of v0, /device:TPU:0, one launch (start us, length us, event | category | flops | bytes accessed | tf_op | source)
XLA Modules:
  0.0 1313.2 jit_solution(7243004674187600519)
XLA Ops:
  9.4 22.5 %all-gather = bf16[8,1,128]{2,1,0:T(2,128)(2,1)S(1)} all-gather(bf16[1,1,128]{2,1,0:T(2,128)(2,1)} %bitcast.228), channel_id=1, replica_groups=mesh['fsdp'=8,'seq'=4] {'fsdp'}, dimensions={0}, use_global_device_ids=true | all-gather | bytes 2304 | tf_op jit(solution)/shard_map/all_gather | solution.py:138
  33.7 78.3 %all-gather.7.cloned.1.call-done = bf16[1024,3072]{1,0:T(8,128)(2,1)} async-done(((bf16[128,3072]{1,0:T(8,128)(2,1)}), bf16[1024,3072]{1,0:T(8,128)(2,1)}) %all-gather.7.cloned.1.call-update) | async-done | bytes 6291472 | tf_op jit(solution)/shard_map/all_gather | solution.py:139
  147.1 58.9 %all-to-all-done = bf16[1,640,3,1024]{1,2,0,3:T(4,128)(2,1)} async-done(((bf16[1,640,3,1024]{1,2,0,3:T(4,128)(2,1)}), bf16[1,640,3,1024]{1,2,0,3:T(4,128)(2,1)}, u32[]{:S(2)}, u32[]{:S(2)}) %all-to-all-start) | async-done | bytes 3932192 | tf_op jit(solution)/shard_map/all_to_all | solution.py:161
  228.4 93.1 %while.45 = (s32[]{:T(128)}, bf16[5,512,256]{2,1,0:T(8,128)(2,1)}, f32[5,4,512]{2,1,0:T(4,128)}, bf16[5,512,4,64]{1,3,2,0:T(8,128)(2,1)}, bf16[2560,4,64]{0,2,1:...) while((s32[]{:T(128)}, bf16[5,512,256]{2,1,0:T(8,128)(2,1)}, f32[5,4,512]{2,1,0:T(4,128)}, ...), condition=%wide.region_5.0_spmd, body=%wide.region_2.5_spmd.sunk | while | flops 1389492224 | bytes 67174496 | solution.py:81
  326.2 14.1 %reduce.1 = bf16[2560,256]{1,0:T(8,128)(2,1)} reduce(bf16[2560,1,256]{2,1,0:T(2,128)(2,1)S(1)} %bitcast.202, bf16[]{:T(256)} %broadcast.257), dimensions={1}, to_apply=%bitcast.158.reduce_sub_computation | reduce | bytes 2621442
  347.5 17.7 %all-gather.1 = bf16[8,1,128]{2,1,0:T(2,128)(2,1)S(1)} all-gather(bf16[1,1,128]{2,1,0:T(2,128)(2,1)S(1)} %bitcast.229), channel_id=1, replica_groups=mesh['fsdp'=8,'seq'=4] {'fsdp'}, dimensions={0}, use_global_device_ids=true | all-gather | bytes 2304 | tf_op jit(solution)/shard_map/all_gather | solution.py:141
  377.1 15.1 %fusion.73 = f32[640,5248]{1,0:T(8,128)} fusion(bf16[1024,5248]{1,0:T(8,128)(2,1)} %all-gather.11.cloned.1.call-done, f32[640,1024]{1,0:T(8,128)} %copy-done.7, f32[1024]{0:T(1024)S(1)} %bitcast.224, f32[640]{0:T(1024)S(1)} %fusion.67, f32[640]{0:T(1024)S(1)} %broadcast_multiply_fusion.1), kind=kOutput, calls=%fused_computation.125 | convolution fusion | flops 6881280000 | bytes 26813440 | tf_op jit(solution)/shard_map/dot_general | solution.py:168
  392.1 12.3 all-gather.13.cloned.1.call-done
  404.5 14.9 %add_convert_fusion = (bf16[640,2624]{1,0:T(8,128)(2,1)S(1)}, bf16[640,2624]{1,0:T(8,128)(2,1)}, bf16[640,2624]{1,0:T(8,128)(2,1)}) fusion(f32[640,5248]{1,0:T(8,128)} %fusion.73, bf16[2624,1024]{1,0:T(8,128)(2,1)} %all-gather.13.cloned.1.call-done, bf16[1,640,1024]{2,1,0:T(8,128)(2,1)} %param.13), kind=kOutput, calls=%fused_computation.48 | convolution fusion | flops 3471237120 | bytes 30195712 | tf_op jit(solution)/shard_map/dot_general | solution.py:51
  419.4 14.6 %multiply_reduce_fusion.2 = (bf16[1024]{0:T(1024)(128)(2,1)}, f32[640]{0:T(1024)S(1)}, f32[640,1024]{1,0:T(8,128)S(1)}) fusion(f32[640,1024]{1,0:T(8,128)S(1)} %copy-done.8, f32[640]{0:T(1024)S(1)} %fusion.67, f32[640]{0:T(1024)S(1)} %broadcast_multiply_fusion.1, f32[1024]{0:T(1024)S(1)} %bitcast.225, bf16[1024,5248]{1,0:T(8,128)(2,1)} %all-gather.11.cloned.1.call-done, ...), kind=kOutput, calls=%fused_computation.88 | convolution fusion | flops 6896679424 | bytes 22722048 | tf_op jit(solution)/shard_map/dot_general | solution.py:51
  490.0 323.5 %while.46 = (s32[]{:T(128)}, f32[2560,4,64]{0,2,1:T(8,128)}, f32[2560,4,64]{0,2,1:T(8,128)}, bf16[5,512,4,64]{1,3,2,0:T(8,128)(2,1)}, bf16[5,512,4,64]{1,3,2,0:T...) while((s32[]{:T(128)}, f32[2560,4,64]{0,2,1:T(8,128)}, ...), condition=%wide.region_12.13_spmd.clone, body=%wide.region_10.12_spmd.clone.sunk | while | flops 3421763584 | bytes 173334672 | solution.py:119
  502.2 12.6 fusion.132
  514.8 14.7 %multiply_reduce_fusion.8 = (f32[4,512]{1,0:T(4,128)S(1)}, f32[4,512,2560]{2,1,0:T(8,128)}) fusion(f32[4,512,2560]{2,1,0:T(8,128)} %fusion.130, f32[4,512]{1,0:T(4,128)S(1)} %dynamic-slice_bitcast_fusion.2, bf16[2560,4,64]{0,2,1:T(8,128)(2,1)} %get-tuple-element.413, bf16[5,512,4,64]{1,3,2,0:T(8,128)(2,1)} %get-tuple-element.412, s32[]{:T(128)S(6)} %copy.94), kind=kOutput, calls=%fused_computation.14.clone.1 | convolution fusion | flops 692058112 | bytes 43532292 | tf_op jit(solution)/shard_map/while/body/eval_jaxpr/while/body/eval_jaxpr/qhd,khd->hqk/dot_general | solution.py:102
  529.5 15.1 %multiply_convert_fusion.7 = bf16[4,512,2560]{2,1,0:T(8,128)(2,1)S(1)} fusion(f32[4,512,2560]{2,1,0:T(8,128)} %get-tuple-element.360, f32[4,512,2560]{2,1,0:T(8,128)} %fusion.130, f32[4,512]{1,0:T(4,128)S(1)} %get-tuple-element.361, f32[4,512]{1,0:T(4,128)S(1)} %dynamic-slice_bitcast_fusion.2), kind=kLoop, calls=%fused_computation.13.clone.1 | loop fusion | flops 26214400 | bytes 52445184 | tf_op jit(solution)/shard_map/while/body/eval_jaxpr/while/body/eval_jaxpr/convert_element_type | solution.py:106
  566.6 13.6 %fusion.132 = f32[2560,4,64]{0,2,1:T(8,128)} fusion(f32[4,512,2560]{2,1,0:T(8,128)} %fusion.130, f32[4,512]{1,0:T(4,128)S(1)} %dynamic-slice_bitcast_fusion.2, f32[2560,4,64]{0,2,1:T(8,128)} %get-tuple-element.396, pred[]{:T(512)S(6)} %compare.5, bf16[5,512,4,64]{1,3,2,0:T(8,128)(2,1)} %get-tuple-element.412, s32[]{:T(128)S(6)} %copy.94), kind=kOutput, calls=%fused_computation.24.clone.1 | convolution fusion | flops 688128000 | bytes 26484740 | tf_op jit(solution)/shard_map/while/body/eval_jaxpr/while/body/eval_jaxpr/hqk,qhd->khd/dot_general | solution.py:99
  580.2 14.3 %multiply_reduce_fusion.8 = (f32[4,512]{1,0:T(4,128)S(1)}, f32[4,512,2560]{2,1,0:T(8,128)}) fusion(f32[4,512,2560]{2,1,0:T(8,128)} %fusion.130, f32[4,512]{1,0:T(4,128)S(1)} %dynamic-slice_bitcast_fusion.2, bf16[2560,4,64]{0,2,1:T(8,128)(2,1)} %get-tuple-element.413, bf16[5,512,4,64]{1,3,2,0:T(8,128)(2,1)} %get-tuple-element.412, s32[]{:T(128)S(6)} %copy.94), kind=kOutput, calls=%fused_computation.14.clone.1 | convolution fusion | flops 692058112 | bytes 43532292 | tf_op jit(solution)/shard_map/while/body/eval_jaxpr/while/body/eval_jaxpr/qhd,khd->hqk/dot_general | solution.py:102
  594.4 14.7 %multiply_convert_fusion.7 = bf16[4,512,2560]{2,1,0:T(8,128)(2,1)S(1)} fusion(f32[4,512,2560]{2,1,0:T(8,128)} %get-tuple-element.360, f32[4,512,2560]{2,1,0:T(8,128)} %fusion.130, f32[4,512]{1,0:T(4,128)S(1)} %get-tuple-element.361, f32[4,512]{1,0:T(4,128)S(1)} %dynamic-slice_bitcast_fusion.2), kind=kLoop, calls=%fused_computation.13.clone.1 | loop fusion | flops 26214400 | bytes 52445184 | tf_op jit(solution)/shard_map/while/body/eval_jaxpr/while/body/eval_jaxpr/convert_element_type | solution.py:106
  631.8 13.3 %fusion.132 = f32[2560,4,64]{0,2,1:T(8,128)} fusion(f32[4,512,2560]{2,1,0:T(8,128)} %fusion.130, f32[4,512]{1,0:T(4,128)S(1)} %dynamic-slice_bitcast_fusion.2, f32[2560,4,64]{0,2,1:T(8,128)} %get-tuple-element.396, pred[]{:T(512)S(6)} %compare.5, bf16[5,512,4,64]{1,3,2,0:T(8,128)(2,1)} %get-tuple-element.412, s32[]{:T(128)S(6)} %copy.94), kind=kOutput, calls=%fused_computation.24.clone.1 | convolution fusion | flops 688128000 | bytes 26484740 | tf_op jit(solution)/shard_map/while/body/eval_jaxpr/while/body/eval_jaxpr/hqk,qhd->khd/dot_general | solution.py:99
  645.1 14.2 %multiply_reduce_fusion.8 = (f32[4,512]{1,0:T(4,128)S(1)}, f32[4,512,2560]{2,1,0:T(8,128)}) fusion(f32[4,512,2560]{2,1,0:T(8,128)} %fusion.130, f32[4,512]{1,0:T(4,128)S(1)} %dynamic-slice_bitcast_fusion.2, bf16[2560,4,64]{0,2,1:T(8,128)(2,1)} %get-tuple-element.413, bf16[5,512,4,64]{1,3,2,0:T(8,128)(2,1)} %get-tuple-element.412, s32[]{:T(128)S(6)} %copy.94), kind=kOutput, calls=%fused_computation.14.clone.1 | convolution fusion | flops 692058112 | bytes 43532292 | tf_op jit(solution)/shard_map/while/body/eval_jaxpr/while/body/eval_jaxpr/qhd,khd->hqk/dot_general | solution.py:102
  659.3 14.3 %multiply_convert_fusion.7 = bf16[4,512,2560]{2,1,0:T(8,128)(2,1)S(1)} fusion(f32[4,512,2560]{2,1,0:T(8,128)} %get-tuple-element.360, f32[4,512,2560]{2,1,0:T(8,128)} %fusion.130, f32[4,512]{1,0:T(4,128)S(1)} %get-tuple-element.361, f32[4,512]{1,0:T(4,128)S(1)} %dynamic-slice_bitcast_fusion.2), kind=kLoop, calls=%fused_computation.13.clone.1 | loop fusion | flops 26214400 | bytes 52445184 | tf_op jit(solution)/shard_map/while/body/eval_jaxpr/while/body/eval_jaxpr/convert_element_type | solution.py:106
  696.3 13.3 %fusion.132 = f32[2560,4,64]{0,2,1:T(8,128)} fusion(f32[4,512,2560]{2,1,0:T(8,128)} %fusion.130, f32[4,512]{1,0:T(4,128)S(1)} %dynamic-slice_bitcast_fusion.2, f32[2560,4,64]{0,2,1:T(8,128)} %get-tuple-element.396, pred[]{:T(512)S(6)} %compare.5, bf16[5,512,4,64]{1,3,2,0:T(8,128)(2,1)} %get-tuple-element.412, s32[]{:T(128)S(6)} %copy.94), kind=kOutput, calls=%fused_computation.24.clone.1 | convolution fusion | flops 688128000 | bytes 26484740 | tf_op jit(solution)/shard_map/while/body/eval_jaxpr/while/body/eval_jaxpr/hqk,qhd->khd/dot_general | solution.py:99
  709.6 14.2 %multiply_reduce_fusion.8 = (f32[4,512]{1,0:T(4,128)S(1)}, f32[4,512,2560]{2,1,0:T(8,128)}) fusion(f32[4,512,2560]{2,1,0:T(8,128)} %fusion.130, f32[4,512]{1,0:T(4,128)S(1)} %dynamic-slice_bitcast_fusion.2, bf16[2560,4,64]{0,2,1:T(8,128)(2,1)} %get-tuple-element.413, bf16[5,512,4,64]{1,3,2,0:T(8,128)(2,1)} %get-tuple-element.412, s32[]{:T(128)S(6)} %copy.94), kind=kOutput, calls=%fused_computation.14.clone.1 | convolution fusion | flops 692058112 | bytes 43532292 | tf_op jit(solution)/shard_map/while/body/eval_jaxpr/while/body/eval_jaxpr/qhd,khd->hqk/dot_general | solution.py:102
  723.8 14.3 %multiply_convert_fusion.7 = bf16[4,512,2560]{2,1,0:T(8,128)(2,1)S(1)} fusion(f32[4,512,2560]{2,1,0:T(8,128)} %get-tuple-element.360, f32[4,512,2560]{2,1,0:T(8,128)} %fusion.130, f32[4,512]{1,0:T(4,128)S(1)} %get-tuple-element.361, f32[4,512]{1,0:T(4,128)S(1)} %dynamic-slice_bitcast_fusion.2), kind=kLoop, calls=%fused_computation.13.clone.1 | loop fusion | flops 26214400 | bytes 52445184 | tf_op jit(solution)/shard_map/while/body/eval_jaxpr/while/body/eval_jaxpr/convert_element_type | solution.py:106
  760.8 13.3 %fusion.132 = f32[2560,4,64]{0,2,1:T(8,128)} fusion(f32[4,512,2560]{2,1,0:T(8,128)} %fusion.130, f32[4,512]{1,0:T(4,128)S(1)} %dynamic-slice_bitcast_fusion.2, f32[2560,4,64]{0,2,1:T(8,128)} %get-tuple-element.396, pred[]{:T(512)S(6)} %compare.5, bf16[5,512,4,64]{1,3,2,0:T(8,128)(2,1)} %get-tuple-element.412, s32[]{:T(128)S(6)} %copy.94), kind=kOutput, calls=%fused_computation.24.clone.1 | convolution fusion | flops 688128000 | bytes 26484740 | tf_op jit(solution)/shard_map/while/body/eval_jaxpr/while/body/eval_jaxpr/hqk,qhd->khd/dot_general | solution.py:99
  774.1 14.2 %multiply_reduce_fusion.8 = (f32[4,512]{1,0:T(4,128)S(1)}, f32[4,512,2560]{2,1,0:T(8,128)}) fusion(f32[4,512,2560]{2,1,0:T(8,128)} %fusion.130, f32[4,512]{1,0:T(4,128)S(1)} %dynamic-slice_bitcast_fusion.2, bf16[2560,4,64]{0,2,1:T(8,128)(2,1)} %get-tuple-element.413, bf16[5,512,4,64]{1,3,2,0:T(8,128)(2,1)} %get-tuple-element.412, s32[]{:T(128)S(6)} %copy.94), kind=kOutput, calls=%fused_computation.14.clone.1 | convolution fusion | flops 692058112 | bytes 43532292 | tf_op jit(solution)/shard_map/while/body/eval_jaxpr/while/body/eval_jaxpr/qhd,khd->hqk/dot_general | solution.py:102
  788.3 14.3 %multiply_convert_fusion.7 = bf16[4,512,2560]{2,1,0:T(8,128)(2,1)S(1)} fusion(f32[4,512,2560]{2,1,0:T(8,128)} %get-tuple-element.360, f32[4,512,2560]{2,1,0:T(8,128)} %fusion.130, f32[4,512]{1,0:T(4,128)S(1)} %get-tuple-element.361, f32[4,512]{1,0:T(4,128)S(1)} %dynamic-slice_bitcast_fusion.2), kind=kLoop, calls=%fused_computation.13.clone.1 | loop fusion | flops 26214400 | bytes 52445184 | tf_op jit(solution)/shard_map/while/body/eval_jaxpr/while/body/eval_jaxpr/convert_element_type | solution.py:106
  834.2 63.3 %all_to_all.54 = bf16[1,2560,3,256]{3,2,0,1:T(4,128)(2,1)S(1)} all-to-all(bf16[1,2560,3,256]{3,2,0,1:T(4,128)(2,1)} %copy.65), channel_id=1, replica_groups=mesh['fsdp'=8,'seq'=4] {'seq'}, dimensions={1} | all-to-all | bytes 7864320 | tf_op jit(solution)/shard_map/all_to_all | solution.py:199
  929.3 15.7 %convolution_convert_fusion = bf16[1024,5248]{1,0:T(8,128)(2,1)} fusion(bf16[640,2624]{1,0:T(8,128)(2,1)} %get-tuple-element.246, bf16[640,2624]{1,0:T(8,128)(2,1)} %copy-done.41, f32[640,1024]{1,0:T(8,128)} %copy-done.7, f32[1024]{0:T(1024)S(1)} %bitcast.227, f32[640]{0:T(1024)S(1)} %copy-done.36, f32[640]{0:T(1024)S(1)} %copy-done.24), kind=kOutput, calls=%fused_computation.44 | convolution fusion | flops 6900088832 | bytes 20096000 | tf_op jit(solution)/shard_map/dot_general | solution.py:45
  956.3 88.0 %reduce-scatter.5.cloned.1.call-done = bf16[128,3072]{1,0:T(8,128)(2,1)} async-done(((bf16[1024,3072]{1,0:T(8,128)(2,1)}), bf16[128,3072]{1,0:T(8,128)(2,1)}) %reduce-scatter.5.cloned.1.call-update) | async-done | bytes 786448 | tf_op jit(solution)/shard_map/reduce_scatter | solution.py:216
  1044.3 185.0 %reduce-scatter.9.cloned.1.call-done = bf16[128,5248]{1,0:T(8,128)(2,1)} async-done(((bf16[1024,5248]{1,0:T(8,128)(2,1)}), bf16[128,5248]{1,0:T(8,128)(2,1)}) %reduce-scatter.9.cloned.1.call-update) | async-done | bytes 1343504 | tf_op jit(solution)/shard_map/reduce_scatter | solution.py:222
  1238.9 19.6 %all-reduce.4 = (bf16[1024]{0:T(1024)(128)(2,1)S(1)}, bf16[1024]{0:T(1024)(128)(2,1)S(1)}) all-reduce(bf16[1024]{0:T(1024)(128)(2,1)S(1)} %get-tuple-element.199, bf16[1024]{0:T(1024)(128)(2,1)S(1)} %copy-done.37), channel_id=2, replica_groups=mesh['fsdp'=8,'seq'=4] {'fsdp'}, use_global_device_ids=true, to_apply=%region_16.17.clone | all-reduce | flops 2048 | bytes 8192
  1269.7 29.3 %all-reduce.9.cloned.1.call-done = (bf16[128,3072]{1,0:T(8,128)(2,1)}, bf16[128,1024]{1,0:T(8,128)(2,1)}, bf16[128,5248]{1,0:T(8,128)(2,1)}, bf16[328,1024]{1,0:T(8,128)(2,1)}) async-done(((bf16[128,3072]{1,0:T(8,128)(2,1)}, bf16[128,1024]{1,0:T(8,128)(2,1)}, bf16[128,5248]{1,0:T(8,128)(2,1)}, bf16[328,1024]{1,0:T(8,128)(2,1)}), (bf16[128,3072]{1,0:T(8,128)(2,1)}, bf16[128,1024]{1,0:T(8,128)(2,1)}, ...) | async-done | bytes 3063824 | tf_op jit(solution)/shard_map/psum | solution.py:232
  (250 shorter events, 437.6 us)
Async XLA Ops:
  7.2 25.2 %copy-start.3 = (bf16[1,640,1024]{2,1,0:T(8,128)(2,1)S(1)}, bf16[1,640,1024]{2,1,0:T(8,128)(2,1)}, u32[]{:S(2)}) copy-start(bf16[1,640,1024]{2,1,0:T(8,128)(2,1)} %param.12) | copy-start | bytes 3932164
  7.2 104.8 %all-gather.7.cloned.1.call-start = ((), (), s32[]{:S(2)}) async-start(), calls=%async_computation.8 | async-start | bytes 7077888 | tf_op jit(solution)/shard_map/all_gather | solution.py:139
  7.9 363.6 %all-gather.9.cloned.1.call-start = ((), (), s32[]{:S(2)}) async-start(), calls=%async_computation.9 | async-start | bytes 2359296 | tf_op jit(solution)/shard_map/all_gather | solution.py:140
  8.7 368.4 %all-gather.11.cloned.1.call-start = ((), (), s32[]{:S(2)}) async-start(), calls=%async_computation.10 | async-start | bytes 12091392 | tf_op jit(solution)/shard_map/all_gather | solution.py:142
  31.9 88.7 %copy-start.27 = (f32[8,1,128]{2,1,0:T(1,128)}, f32[8,1,128]{2,1,0:T(1,128)S(1)}, u32[]{:S(2)}) copy-start(f32[8,1,128]{2,1,0:T(1,128)S(1)} %convert_element_type.213) | copy-start | bytes 12292
  32.3 98.8 %copy-start.14 = (f32[640,64]{0,1:T(8,128)}, f32[640,64]{0,1:T(8,128)S(1)}, u32[]{:S(2)}) copy-start(f32[640,64]{0,1:T(8,128)S(1)} %get-tuple-element.255) | copy-start | bytes 491524
  32.4 98.8 %copy-start.16 = (f32[640,64]{0,1:T(8,128)}, f32[640,64]{0,1:T(8,128)S(1)}, u32[]{:S(2)}) copy-start(f32[640,64]{0,1:T(8,128)S(1)} %get-tuple-element.256) | copy-start | bytes 491524
  32.6 88.0 %copy-start.21 = (f32[640]{0:T(1024)}, f32[640]{0:T(1024)S(1)}, u32[]{:S(2)}) copy-start(f32[640]{0:T(1024)S(1)} %broadcast_multiply_fusion.2) | copy-start | bytes 7684
  33.7 87.0 %copy-start.29 = (f32[640]{0:T(1024)}, f32[640]{0:T(1024)S(1)}, u32[]{:S(2)}) copy-start(f32[640]{0:T(1024)S(1)} %fusion.66) | copy-start | bytes 7684
  141.4 64.5 %all-to-all-start = ((bf16[1,640,3,1024]{1,2,0,3:T(4,128)(2,1)}), bf16[1,640,3,1024]{1,2,0,3:T(4,128)(2,1)}, u32[]{:S(2)}, u32[]{:S(2)}) async-start(bf16[1,640,3,1024]{1,2,0,3:T(4,128)(2,1)} %pad_maximum_fusion.1), calls=%async_computation | async-start | bytes 10485760 | tf_op jit(solution)/shard_map/all_to_all | solution.py:161
  146.5 258.0 %all-gather.13.cloned.1.call-start = ((), (), s32[]{:S(2)}) async-start(), calls=%async_computation.11 | async-start | bytes 6045696 | tf_op jit(solution)/shard_map/all_gather | solution.py:143
  340.3 7.2 copy-start.38
  343.9 21.3 %all-to-all-start.1 = ((bf16[4,2,81920]{2,1,0:T(2,128)(2,1)}), bf16[4,2,81920]{2,1,0:T(2,128)(2,1)S(1)}, u32[]{:S(2)}, u32[]{:S(2)}) async-start(bf16[4,2,81920]{2,1,0:T(2,128)(2,1)} %reshape.443), calls=%async_computation.1 | async-start | bytes 2621440 | tf_op jit(solution)/shard_map/all_to_all | solution.py:163
  347.5 608.8 %reduce-scatter.7.cloned.1.call-start = ((), (), s32[]{:S(2)}) async-start(), calls=%async_computation.13 | async-start | bytes 2359296 | tf_op jit(solution)/shard_map/reduce_scatter | solution.py:219
  365.2 68.8 %copy-start.33 = (f32[8,1,128]{2,1,0:T(1,128)}, f32[8,1,128]{2,1,0:T(1,128)S(1)}, u32[]{:S(2)}) copy-start(f32[8,1,128]{2,1,0:T(1,128)S(1)} %convert_element_type.214) | copy-start | bytes 12292
  375.2 58.9 %copy-start.23 = (f32[640]{0:T(1024)}, f32[640]{0:T(1024)S(1)}, u32[]{:S(2)}) copy-start(f32[640]{0:T(1024)S(1)} %broadcast_multiply_fusion.1) | copy-start | bytes 7684
  377.0 57.1 %copy-start.35 = (f32[640]{0:T(1024)}, f32[640]{0:T(1024)S(1)}, u32[]{:S(2)}) copy-start(f32[640]{0:T(1024)S(1)} %fusion.67) | copy-start | bytes 7684
  392.1 27.3 %copy-start.8 = (f32[640,1024]{1,0:T(8,128)S(1)}, f32[640,1024]{1,0:T(8,128)}, u32[]{:S(2)}) copy-start(f32[640,1024]{1,0:T(8,128)} %copy-done.7) | copy-start | bytes 7864324
  419.4 14.6 %copy-start.41 = (bf16[640,2624]{1,0:T(8,128)(2,1)}, bf16[640,2624]{1,0:T(8,128)(2,1)S(1)}, u32[]{:S(2)}) copy-start(bf16[640,2624]{1,0:T(8,128)(2,1)S(1)} %get-tuple-element.245) | copy-start | bytes 10076164
  458.1 8.1 copy-start.12
  461.8 21.6 %all-to-all-start.2 = ((bf16[4,2,81920]{2,1,0:T(2,128)(2,1)}), bf16[4,2,81920]{2,1,0:T(2,128)(2,1)}, u32[]{:S(2)}, u32[]{:S(2)}) async-start(bf16[4,2,81920]{2,1,0:T(2,128)(2,1)} %reshape.445), calls=%async_computation.2 | async-start | bytes 2621440 | tf_op jit(solution)/shard_map/all_to_all | solution.py:197
  466.2 490.1 %reduce-scatter.11.cloned.1.call-start = ((), (), s32[]{:S(2)}) async-start(), calls=%async_computation.15 | async-start | bytes 6045696 | tf_op jit(solution)/shard_map/reduce_scatter | solution.py:225
  474.5 569.8 %reduce-scatter.5.cloned.1.call-start = ((), (), s32[]{:S(2)}) async-start(), calls=%async_computation.12 | async-start | bytes 7077888 | tf_op jit(solution)/shard_map/reduce_scatter | solution.py:216
  813.5 7.7 copy-start
  911.1 5.5 slice-start
  928.7 300.6 %reduce-scatter.9.cloned.1.call-start = ((), (), s32[]{:S(2)}) async-start(), calls=%async_computation.14 | async-start | bytes 12091392 | tf_op jit(solution)/shard_map/reduce_scatter | solution.py:222
  945.0 353.9 %all-reduce.9.cloned.1.call-start = ((), (), s32[]{:S(2)}) async-start(), calls=%async_computation.16 | async-start | bytes 6127616 | tf_op jit(solution)/shard_map/psum | solution.py:232
  1229.3 8.2 copy-start.26
  1229.3 8.2 copy-start.6
  1237.5 28.3 %copy-start.2 = (f32[640,1024]{1,0:T(8,128)S(1)}, f32[640,1024]{1,0:T(8,128)}, u32[]{:S(2)}) copy-start(f32[640,1024]{1,0:T(8,128)} %copy-done.1) | copy-start | bytes 7864324
  1237.5 28.2 %copy-start.32 = (f32[640]{0:T(1024)S(1)}, f32[640]{0:T(1024)}, u32[]{:S(2)}) copy-start(f32[640]{0:T(1024)} %copy-done.31) | copy-start | bytes 7684
  1299.0 5.6 copy-start.18
  (24 other events, 45.5 us)
Sparse Core Ops, SparseCore 0:
  10.2 101.7 all-gather.6
  114.1 47.4 all-gather.8
  163.8 152.5 all-gather.10
  318.4 86.0 all-gather.12
  440.6 66.1 reduce-scatter.6
  510.2 103.5 reduce-scatter.10
  928.8 115.4 reduce-scatter.4
  1048.3 180.8 reduce-scatter.8
  1231.9 67.0 all-reduce.8
where the time goes:
time: 1320 us; the launch traced here: 1310 us
  waiting for transfers between devices  463 us (35%)
  matrix products  413 us (31%)
  other arithmetic  163 us (12%)
  blocking collectives  129 us (10%)
  local copies, waits for them, and re-layouts  116 us (9%)
  between operations  15.6 us (1%)
  starting transfers between devices  13.6 us (1%)
    reduce_scatter x1, waiting for transfers between devices, local(): lax.psum_scatter(gradients[4].astype(jnp.bfloat16), 'fsdp', scatter_dimen...  185 us
    reduce_scatter x1, waiting for transfers between devices, local(): lax.psum_scatter(gradients[2].astype(jnp.bfloat16), 'fsdp', scatter_dimen...  88 us
    dot_general x10, matrix products, one_block(): jnp.einsum('qhd,khd->hqk', q_block, key_rows, preferred_element_type=jnp....  79 us
    all_gather x1, waiting for transfers between devices, local(): lax.all_gather(w_qkv, 'fsdp', axis=0, tiled=True)  78.3 us
    convert_element_type x5, other arithmetic, one_block(): score_grad = (probs * (prob_grad - inner)).astype(jnp.bfloat16)  72.9 us
    dot_general x5, matrix products, one_block(): jnp.einsum('qhd,khd->hqk', g_block, value_rows, preferred_element_type=jn...  71.4 us
    dot_general x5, matrix products, one_block(): jnp.einsum('hqk,qhd->khd', probs.astype(jnp.bfloat16), g_block, preferred...  66 us
    all_to_all x1, blocking collectives, local(): lax.all_to_all(rotated_grad, 'seq', split_axis=1, concat_axis=3, tiled=True)  63.3 us
  transfers between devices with their start and end apart: 12, of which 7 were waited for; matrix products, arithmetic and copies ran while one was open for 49% of the time, Pallas kernels for 0%

commit v1 on v0

--- a/solution.py
+++ b/solution.py
@@ -134,9 +134,24 @@
 def local(activations, cotangent, gain_attn, w_qkv, w_attn_out, gain_mlp, w_in, w_mlp_out):
     local_seqs, positions, width = activations.shape
     row_count = local_seqs * positions
+
+    def _match_tails(inp, named_axis):
+        val = jax.lax.axis_size(named_axis)
+        k_now, low = (val, jax.lax.axis_index(named_axis))
+        back, met_up = (inp, 1)
+        while met_up < k_now:
+            current_value = jax.lax.ppermute(
+                back, axis_name=named_axis, perm=[(it, it ^ met_up) for it in range(k_now)]
+            )
+            finding = jnp.concatenate([back, current_value], axis=0)
+            built = jnp.concatenate([current_value, back], axis=0)
+            back = jnp.where(low & met_up == 0, finding, built)
+            met_up = 2 * met_up
+        return back
+
     gathered = (
         lax.all_gather(gain_attn, "fsdp", axis=0, tiled=True),
-        lax.all_gather(w_qkv, "fsdp", axis=0, tiled=True),
+        _match_tails(w_qkv, "fsdp"),
         lax.all_gather(w_attn_out, "fsdp", axis=0, tiled=True),
         lax.all_gather(gain_mlp, "fsdp", axis=0, tiled=True),
         lax.all_gather(w_in, "fsdp", axis=0, tiled=True),

time: 1320 us -> 1650 us (1.25)
  waiting for transfers between devices: 463 us -> 698 us
  blocking collectives: 129 us -> 220 us
    ppermute x0 -> x3, waiting for transfers between devices: none -> 226 us  [_match_tails(): jax.lax.ppermute(back, axis_name=named_axis, perm=[(it, it ^ met_up) for...]
    all_gather x1, blocking collectives: 22.5 us -> 105 us  [local(): lax.all_gather(gain_attn, 'fsdp', axis=0, tiled=True)]
    all_gather x1, waiting for transfers between devices: 78.3 us -> 100 us  [local(): lax.all_gather(w_qkv, 'fsdp', axis=0, tiled=True)]
  transfers between devices with their start and end apart: 12 -> 15, of which waited for: 7 -> 9; matrix products, arithmetic and copies ran while one was open for 49% -> 39% of each run, Pallas kernels for 0% -> 0%
where the time goes in v1:
time: 1650 us
  waiting for transfers between devices  698 us (42%)
  matrix products  411 us (25%)
  blocking collectives  220 us (13%)
  other arithmetic  177 us (11%)
  local copies, waits for them, and re-layouts  107 us (6%)
  starting transfers between devices  20.5 us (1%)
    ppermute x3, waiting for transfers between devices, _match_tails(): jax.lax.ppermute(back, axis_name=named_axis, perm=[(it, it ^ met_up) for...  226 us
    reduce_scatter x1, waiting for transfers between devices, local(): lax.psum_scatter(gradients[4].astype(jnp.bfloat16), 'fsdp', scatter_dimen...  185 us
    all_gather x1, blocking collectives, local(): lax.all_gather(gain_attn, 'fsdp', axis=0, tiled=True)  105 us
    all_gather x1, waiting for transfers between devices, local(): lax.all_gather(w_qkv, 'fsdp', axis=0, tiled=True)  100 us
    reduce_scatter x1, waiting for transfers between devices, local(): lax.psum_scatter(gradients[2].astype(jnp.bfloat16), 'fsdp', scatter_dimen...  87.7 us
    dot_general x10, matrix products, one_block(): jnp.einsum('qhd,khd->hqk', q_block, key_rows, preferred_element_type=jnp....  79.1 us
    convert_element_type x5, other arithmetic, one_block(): score_grad = (probs * (prob_grad - inner)).astype(jnp.bfloat16)  72.9 us
    dot_general x5, matrix products, one_block(): jnp.einsum('qhd,khd->hqk', g_block, value_rows, preferred_element_type=jn...  71.7 us
  transfers between devices with their start and end apart: 15, of which 9 were waited for; matrix products, arithmetic and copies ran while one was open for 39% of the time, Pallas kernels for 0%

profile of v1, /device:TPU:0, one launch (start us, length us, event | category | flops | bytes accessed | tf_op | source)
XLA Modules:
  0.0 1649.5 jit_solution(17928021364418721769)
XLA Ops:
  13.2 20.5 %collective-permute-done = bf16[128,3072]{0,1:T(8,128)(2,1)} collective-permute-done((bf16[128,3072]{0,1:T(8,128)(2,1)S(1)}, bf16[128,3072]{0,1:T(8,128)(2,1)}, u32[]{:S(2)}, u32[]{:S(2)}) %collective-permute-start) | collective-permute-done | bytes 786464 | tf_op jit(solution)/shard_map/ppermute | solution.py:143
  37.4 50.9 %collective-permute-done.1 = bf16[256,3072]{0,1:T(8,128)(2,1)} collective-permute-done((bf16[256,3072]{0,1:T(8,128)(2,1)S(1)}, bf16[256,3072]{0,1:T(8,128)(2,1)}, u32[]{:S(2)}, u32[]{:S(2)}) %collective-permute-start.1) | collective-permute-done | bytes 1572896 | tf_op jit(solution)/shard_map/ppermute | solution.py:143
  94.5 104.8 %all-gather = bf16[8,1,128]{2,1,0:T(2,128)(2,1)S(1)} all-gather(bf16[1,1,128]{2,1,0:T(2,128)(2,1)S(1)} %bitcast.228), channel_id=1, replica_groups=mesh['fsdp'=8,'seq'=4] {'fsdp'}, dimensions={0}, use_global_device_ids=true | all-gather | bytes 2304 | tf_op jit(solution)/shard_map/all_gather | solution.py:153
  200.5 154.3 %collective-permute-done.2 = bf16[512,3072]{0,1:T(8,128)(2,1)} collective-permute-done((bf16[512,3072]{0,1:T(8,128)(2,1)}, bf16[512,3072]{0,1:T(8,128)(2,1)}, u32[]{:S(2)}, u32[]{:S(2)}) %collective-permute-start.2) | collective-permute-done | bytes 3145760 | tf_op jit(solution)/shard_map/ppermute | solution.py:143
  387.2 58.7 %all-to-all-done = bf16[1,640,3,1024]{1,2,0,3:T(4,128)(2,1)} async-done(((bf16[1,640,3,1024]{1,2,0,3:T(4,128)(2,1)}), bf16[1,640,3,1024]{1,2,0,3:T(4,128)(2,1)}, u32[]{:S(2)}, u32[]{:S(2)}) %all-to-all-start) | async-done | bytes 3932192 | tf_op jit(solution)/shard_map/all_to_all | solution.py:176
  468.3 93.1 %while.45 = (s32[]{:T(128)}, bf16[5,512,256]{2,1,0:T(8,128)(2,1)}, f32[5,4,512]{2,1,0:T(4,128)}, bf16[5,512,4,64]{1,3,2,0:T(8,128)(2,1)}, bf16[2560,4,64]{0,2,1:...) while((s32[]{:T(128)}, bf16[5,512,256]{2,1,0:T(8,128)(2,1)}, f32[5,4,512]{2,1,0:T(4,128)}, ...), condition=%wide.region_5.6_spmd, body=%wide.region_2.5_spmd.sunk | while | flops 1389492224 | bytes 67174496 | solution.py:81
  566.0 14.1 reduce.1
  587.4 27.0 %all-gather.1 = bf16[8,1,128]{2,1,0:T(2,128)(2,1)S(1)} all-gather(bf16[1,1,128]{2,1,0:T(2,128)(2,1)S(1)} %bitcast.229), channel_id=1, replica_groups=mesh['fsdp'=8,'seq'=4] {'fsdp'}, dimensions={0}, use_global_device_ids=true | all-gather | bytes 2304 | tf_op jit(solution)/shard_map/all_gather | solution.py:156
  626.2 15.0 fusion.73
  641.3 15.2 add_convert_fusion
  656.5 14.6 multiply_reduce_fusion.2
  726.9 323.7 %while.46 = (s32[]{:T(128)}, f32[2560,4,64]{0,2,1:T(8,128)}, f32[2560,4,64]{0,2,1:T(8,128)}, bf16[5,512,4,64]{1,3,2,0:T(8,128)(2,1)}, bf16[5,512,4,64]{1,3,2,0:T...) while((s32[]{:T(128)}, f32[2560,4,64]{0,2,1:T(8,128)}, ...), condition=%wide.region_12.13_spmd.clone, body=%wide.region_10.12_spmd.clone.sunk | while | flops 3421763584 | bytes 173334672 | solution.py:119
  751.8 14.7 multiply_reduce_fusion.8
  766.5 15.1 multiply_convert_fusion.7
  803.6 13.6 fusion.132
  817.2 14.3 multiply_reduce_fusion.8
  831.5 14.7 multiply_convert_fusion.7
  868.9 13.2 fusion.132
  882.1 14.3 multiply_reduce_fusion.8
  896.4 14.3 multiply_convert_fusion.7
  946.6 14.2 multiply_reduce_fusion.8
  960.9 14.3 multiply_convert_fusion.7
  997.9 13.2 fusion.132
  1011.1 14.2 multiply_reduce_fusion.8
  1025.4 14.3 multiply_convert_fusion.7
  1071.4 63.3 %all_to_all.54 = bf16[1,2560,3,256]{3,2,0,1:T(4,128)(2,1)S(1)} all-to-all(bf16[1,2560,3,256]{3,2,0,1:T(4,128)(2,1)} %copy.71), channel_id=1, replica_groups=mesh['fsdp'=8,'seq'=4] {'seq'}, dimensions={1} | all-to-all | bytes 7864320 | tf_op jit(solution)/shard_map/all_to_all | solution.py:214
  1166.4 15.7 convolution_convert_fusion
  1193.6 87.7 %reduce-scatter.5.cloned.1.call-done = bf16[128,3072]{1,0:T(8,128)(2,1)} async-done(((bf16[1024,3072]{1,0:T(8,128)(2,1)}), bf16[128,3072]{1,0:T(8,128)(2,1)}) %reduce-scatter.5.cloned.1.call-update) | async-done | bytes 786448 | tf_op jit(solution)/shard_map/reduce_scatter | solution.py:231
  1281.2 184.9 %reduce-scatter.9.cloned.1.call-done = bf16[128,5248]{1,0:T(8,128)(2,1)} async-done(((bf16[1024,5248]{1,0:T(8,128)(2,1)}), bf16[128,5248]{1,0:T(8,128)(2,1)}) %reduce-scatter.9.cloned.1.call-update) | async-done | bytes 1343504 | tf_op jit(solution)/shard_map/reduce_scatter | solution.py:237
  1466.2 100.3 %all-gather.13.cloned.1.call-done = bf16[1024,3072]{1,0:T(8,128)(2,1)} async-done(((bf16[128,3072]{1,0:T(8,128)(2,1)}), bf16[1024,3072]{1,0:T(8,128)(2,1)}) %all-gather.13.cloned.1.call-update) | async-done | bytes 6291472 | tf_op jit(solution)/shard_map/all_gather | solution.py:193
  1576.1 18.7 %all-reduce.4 = (bf16[1024]{0:T(1024)(128)(2,1)S(1)}, bf16[1024]{0:T(1024)(128)(2,1)S(1)}) all-reduce(bf16[1024]{0:T(1024)(128)(2,1)S(1)} %get-tuple-element.199, bf16[1024]{0:T(1024)(128)(2,1)S(1)} %copy-done.37), channel_id=2, replica_groups=mesh['fsdp'=8,'seq'=4] {'fsdp'}, use_global_device_ids=true, to_apply=%region_16.17.clone | all-reduce | flops 2048 | bytes 8192
  1606.0 29.3 %all-reduce.9.cloned.1.call-done = (bf16[128,3072]{1,0:T(8,128)(2,1)}, bf16[128,1024]{1,0:T(8,128)(2,1)}, bf16[128,5248]{1,0:T(8,128)(2,1)}, bf16[328,1024]{1,0:T(8,128)(2,1)}) async-done(((bf16[128,3072]{1,0:T(8,128)(2,1)}, bf16[128,1024]{1,0:T(8,128)(2,1)}, bf16[128,5248]{1,0:T(8,128)(2,1)}, bf16[328,1024]{1,0:T(8,128)(2,1)}), (bf16[128,3072]{1,0:T(8,128)(2,1)}, bf16[128,1024]{1,0:T(8,128)(2,1)}, ...) | async-done | bytes 3063824 | tf_op jit(solution)/shard_map/psum | solution.py:247
  (261 shorter events, 474.0 us)
Async XLA Ops:
  7.2 613.5 %all-gather.7.cloned.1.call-start = ((), (), s32[]{:S(2)}) async-start(), calls=%async_computation.8 | async-start | bytes 2359296 | tf_op jit(solution)/shard_map/all_gather | solution.py:155
  7.9 618.3 %all-gather.9.cloned.1.call-start = ((), (), s32[]{:S(2)}) async-start(), calls=%async_computation.9 | async-start | bytes 12091392 | tf_op jit(solution)/shard_map/all_gather | solution.py:157
  10.2 23.5 %collective-permute-start = (bf16[128,3072]{0,1:T(8,128)(2,1)S(1)}, bf16[128,3072]{0,1:T(8,128)(2,1)}, u32[]{:S(2)}, u32[]{:S(2)}) collective-permute-start(bf16[128,3072]{0,1:T(8,128)(2,1)S(1)} %copy.55), channel_id=1, source_target_pairs={{0,4},{4,0},{8,12},{12,8},{16,20},{20,16},{24,28},{28,24},{1,5},{5... | collective-permute-start | bytes 2359304 | tf_op jit(solution)/shard_map/ppermute | solution.py:143
  35.6 52.8 %collective-permute-start.1 = (bf16[256,3072]{0,1:T(8,128)(2,1)S(1)}, bf16[256,3072]{0,1:T(8,128)(2,1)}, u32[]{:S(2)}, u32[]{:S(2)}) collective-permute-start(bf16[256,3072]{0,1:T(8,128)(2,1)S(1)} %maximum_select_fusion.2), channel_id=1, source_target_pairs={{0,8},{4,12},{8,0},{12,4},{16,24},{20,28},{24,16},{28,20},{1,9},{5... | collective-permute-start | bytes 4718600 | tf_op jit(solution)/shard_map/ppermute | solution.py:143
  37.4 57.1 %copy-start.38 = (bf16[128]{0:T(256)(128)(2,1)S(1)}, bf16[128]{0:T(256)(128)(2,1)}, u32[]{:S(2)}) copy-start(bf16[128]{0:T(256)(128)(2,1)} %param.14) | copy-start | bytes 772
  37.4 162.3 %copy-start.3 = (bf16[1,640,1024]{2,1,0:T(8,128)(2,1)S(1)}, bf16[1,640,1024]{2,1,0:T(8,128)(2,1)}, u32[]{:S(2)}) copy-start(bf16[1,640,1024]{2,1,0:T(8,128)(2,1)} %param.12) | copy-start | bytes 3932164
  92.2 262.6 %collective-permute-start.2 = (bf16[512,3072]{0,1:T(8,128)(2,1)}, bf16[512,3072]{0,1:T(8,128)(2,1)}, u32[]{:S(2)}, u32[]{:S(2)}) collective-permute-start(bf16[512,3072]{0,1:T(8,128)(2,1)} %maximum_select_fusion.1), channel_id=1, source_target_pairs={{0,16},{4,20},{8,24},{12,28},{16,0},{20,4},{24,8},{28,12},{1,17},{... | collective-permute-start | bytes 9437192 | tf_op jit(solution)/shard_map/ppermute | solution.py:143
  199.3 163.2 %copy-start.27 = (f32[8,1,128]{2,1,0:T(1,128)}, f32[8,1,128]{2,1,0:T(1,128)S(1)}, u32[]{:S(2)}) copy-start(f32[8,1,128]{2,1,0:T(1,128)S(1)} %convert_element_type.213) | copy-start | bytes 12292
  199.7 170.8 %copy-start.14 = (f32[640,64]{0,1:T(8,128)}, f32[640,64]{0,1:T(8,128)S(1)}, u32[]{:S(2)}) copy-start(f32[640,64]{0,1:T(8,128)S(1)} %get-tuple-element.255) | copy-start | bytes 491524
  199.8 170.8 %copy-start.16 = (f32[640,64]{0,1:T(8,128)}, f32[640,64]{0,1:T(8,128)S(1)}, u32[]{:S(2)}) copy-start(f32[640,64]{0,1:T(8,128)S(1)} %get-tuple-element.256) | copy-start | bytes 491524
  200.0 162.6 %copy-start.21 = (f32[640]{0:T(1024)}, f32[640]{0:T(1024)S(1)}, u32[]{:S(2)}) copy-start(f32[640]{0:T(1024)S(1)} %broadcast_multiply_fusion.2) | copy-start | bytes 7684
  200.5 162.1 %copy-start.25 = (f32[640]{0:T(1024)}, f32[640]{0:T(1024)S(1)}, u32[]{:S(2)}) copy-start(f32[640]{0:T(1024)S(1)} %fusion.48) | copy-start | bytes 7684
  200.5 162.1 %copy-start.29 = (f32[640]{0:T(1024)}, f32[640]{0:T(1024)S(1)}, u32[]{:S(2)}) copy-start(f32[640]{0:T(1024)S(1)} %fusion.66) | copy-start | bytes 7684
  381.3 64.5 %all-to-all-start = ((bf16[1,640,3,1024]{1,2,0,3:T(4,128)(2,1)}), bf16[1,640,3,1024]{1,2,0,3:T(4,128)(2,1)}, u32[]{:S(2)}, u32[]{:S(2)}) async-start(bf16[1,640,3,1024]{1,2,0,3:T(4,128)(2,1)} %pad_maximum_fusion.1), calls=%async_computation | async-start | bytes 10485760 | tf_op jit(solution)/shard_map/all_to_all | solution.py:176
  386.4 254.9 %all-gather.11.cloned.1.call-start = ((), (), s32[]{:S(2)}) async-start(), calls=%async_computation.10 | async-start | bytes 6045696 | tf_op jit(solution)/shard_map/all_gather | solution.py:158
  583.8 30.6 %all-to-all-start.1 = ((bf16[4,2,81920]{2,1,0:T(2,128)(2,1)}), bf16[4,2,81920]{2,1,0:T(2,128)(2,1)S(1)}, u32[]{:S(2)}, u32[]{:S(2)}) async-start(bf16[4,2,81920]{2,1,0:T(2,128)(2,1)} %reshape.443), calls=%async_computation.1 | async-start | bytes 2621440 | tf_op jit(solution)/shard_map/all_to_all | solution.py:178
  587.3 606.2 %reduce-scatter.7.cloned.1.call-start = ((), (), s32[]{:S(2)}) async-start(), calls=%async_computation.13 | async-start | bytes 2359296 | tf_op jit(solution)/shard_map/reduce_scatter | solution.py:234
  614.4 56.6 %copy-start.33 = (f32[8,1,128]{2,1,0:T(1,128)}, f32[8,1,128]{2,1,0:T(1,128)S(1)}, u32[]{:S(2)}) copy-start(f32[8,1,128]{2,1,0:T(1,128)S(1)} %convert_element_type.214) | copy-start | bytes 12292
  624.3 46.7 %copy-start.23 = (f32[640]{0:T(1024)}, f32[640]{0:T(1024)S(1)}, u32[]{:S(2)}) copy-start(f32[640]{0:T(1024)S(1)} %broadcast_multiply_fusion.1) | copy-start | bytes 7684
  626.2 44.9 %copy-start.35 = (f32[640]{0:T(1024)}, f32[640]{0:T(1024)S(1)}, u32[]{:S(2)}) copy-start(f32[640]{0:T(1024)S(1)} %fusion.67) | copy-start | bytes 7684
  641.3 15.2 copy-start.8
  656.4 14.6 copy-start.42
  698.9 21.6 %all-to-all-start.2 = ((bf16[4,2,81920]{2,1,0:T(2,128)(2,1)}), bf16[4,2,81920]{2,1,0:T(2,128)(2,1)}, u32[]{:S(2)}, u32[]{:S(2)}) async-start(bf16[4,2,81920]{2,1,0:T(2,128)(2,1)} %reshape.445), calls=%async_computation.2 | async-start | bytes 2621440 | tf_op jit(solution)/shard_map/all_to_all | solution.py:212
  703.2 490.4 %reduce-scatter.11.cloned.1.call-start = ((), (), s32[]{:S(2)}) async-start(), calls=%async_computation.15 | async-start | bytes 6045696 | tf_op jit(solution)/shard_map/reduce_scatter | solution.py:240
  711.5 569.7 %reduce-scatter.5.cloned.1.call-start = ((), (), s32[]{:S(2)}) async-start(), calls=%async_computation.12 | async-start | bytes 7077888 | tf_op jit(solution)/shard_map/reduce_scatter | solution.py:231
  1165.7 300.4 %reduce-scatter.9.cloned.1.call-start = ((), (), s32[]{:S(2)}) async-start(), calls=%async_computation.14 | async-start | bytes 12091392 | tf_op jit(solution)/shard_map/reduce_scatter | solution.py:237
  1182.1 384.4 %all-gather.13.cloned.1.call-start = ((), (), s32[]{:S(2)}) async-start(), calls=%async_computation.11 | async-start | bytes 7077888 | tf_op jit(solution)/shard_map/all_gather | solution.py:193
  1182.8 452.4 %all-reduce.9.cloned.1.call-start = ((), (), s32[]{:S(2)}) async-start(), calls=%async_computation.16 | async-start | bytes 6127616 | tf_op jit(solution)/shard_map/psum | solution.py:247
  1466.2 108.5 %copy-start.26 = (f32[640]{0:T(1024)S(1)}, f32[640]{0:T(1024)}, u32[]{:S(2)}) copy-start(f32[640]{0:T(1024)} %copy-done.25) | copy-start | bytes 7684
  1566.5 8.2 copy-start.6
  1574.6 27.4 %copy-start.2 = (f32[640,1024]{1,0:T(8,128)S(1)}, f32[640,1024]{1,0:T(8,128)}, u32[]{:S(2)}) copy-start(f32[640,1024]{1,0:T(8,128)} %copy-done.1) | copy-start | bytes 7864324
  1574.7 27.4 %copy-start.32 = (f32[640]{0:T(1024)S(1)}, f32[640]{0:T(1024)}, u32[]{:S(2)}) copy-start(f32[640]{0:T(1024)} %copy-done.31) | copy-start | bytes 7684
  (28 other events, 79.6 us)
Sparse Core Ops, SparseCore 0:
  10.1 65.7 all-gather.6
  78.1 281.2 all-gather.8
  389.4 96.5 all-gather.10
  677.5 65.5 reduce-scatter.6
  746.6 103.3 reduce-scatter.10
  1165.9 115.3 reduce-scatter.4
  1285.3 180.8 reduce-scatter.8
  1468.3 98.1 all-gather.12
  1569.1 66.0 all-reduce.8
